TPU v7x, 32 devices: a whole 2x2x4 slice. The times are simulated.
32 devices in a mesh: grid: 4 (over z), orb: 4 (over y, core), pts: 2 (over x).
Axes of the slice: x: 2, y: 2, z: 4, core: 2. Of those that a mesh axis runs over, the one named last changes fastest.
Arguments:
- orbitals: bfloat16 [1024, 2048], P('grid', 'orb'), may hold values from -6 to 6
- points: int32 [8192], replicated, may hold values from 0 to 1023
- fitting: bfloat16 [1024, 8192], P('grid', ('orb', 'pts')), may hold values from -0.0625 to 0.0625
- screened: bfloat16 [8192, 8192], P(('orb', 'pts'), 'grid'), may hold values from -0.0014648438 to 0.0014648438
Outputs:
- exchange_orbitals: float32 [2048, 1024], P(('orb', 'pts'), 'grid')
- exchange_matrix: float32 [2048, 2048], P(('orb', 'pts'), 'grid')
Inputs may be any that keep to these rules, and one draw needn't show every extreme that they name: Grid rows of the window; two points may name the same row.
All inputs are finite; a program needn't handle non-finite values.
Results may differ from a plain program's by a relative error of at most 0.005.
Values may be sent and summed in bfloat16 or wider, within the bound.
A program may use at most 128 MiB of HBM per device.

v0:
```python
import math

import jax
import jax.numpy as jnp
from jax import lax
from jax.sharding import PartitionSpec as P


def per_device(orbitals, points, fitting, screened):
    grid_index = lax.axis_index("grid")
    orb_index = lax.axis_index("orb")
    pts_index = lax.axis_index("pts")
    n_grid = lax.axis_size("grid")
    n_orb = lax.axis_size("orb")
    n_pts = lax.axis_size("pts")
    rows_dev, width_dev = orbitals.shape
    npoints = points.shape[0]
    point_block = npoints // (n_orb * n_pts)
    column_block = npoints // n_grid
    local_rows = points - grid_index * rows_dev
    inside = (local_rows >= 0) & (local_rows < rows_dev)
    clamped = jnp.clip(local_rows, 0, rows_dev - 1)
    taken = jnp.take(orbitals, clamped, axis=0).astype(jnp.float32)
    selected = jnp.where(inside[:, None], taken, jnp.zeros_like(taken))
    picked = lax.psum(selected.astype(jnp.bfloat16), "grid")
    grouped = picked.reshape(n_orb, n_pts, point_block, width_dev)
    own_rows = lax.dynamic_index_in_dim(grouped, pts_index, 1, keepdims=False).reshape(
        n_orb * point_block, width_dev
    )
    point_rows = lax.dynamic_slice_in_dim(picked, grid_index * column_block, column_block, 0)
    rows_full, point_full = (
        lax.all_gather(own_rows, "orb", axis=1, tiled=True),
        lax.all_gather(point_rows, "orb", axis=1, tiled=True),
    )
    own_full = lax.dynamic_slice_in_dim(rows_full, orb_index * point_block, point_block, 0)
    density = lax.dot_general(
        own_full, point_full, (((1,), (1,)), ((), ())), preferred_element_type=jnp.float32
    )
    masked = (density * screened.astype(jnp.float32)).astype(jnp.bfloat16)
    partial_applied = jnp.dot(masked, point_full, preferred_element_type=jnp.float32)
    applied = lax.psum(partial_applied, "grid").astype(jnp.bfloat16)
    terms = lax.psum_scatter(
        -lax.dot_general(
            applied, fitting, (((0,), (1,)), ((), ())), preferred_element_type=jnp.float32
        ),
        ("orb", "pts"),
        scatter_dimension=0,
        tiled=True,
    )
    rounded = terms.astype(jnp.bfloat16)
    partial_matrix = jnp.dot(
        rounded,
        lax.all_gather(orbitals, "orb", axis=1, tiled=True),
        preferred_element_type=jnp.float32,
    )
    summed = lax.psum_scatter(partial_matrix, "grid", scatter_dimension=1, tiled=True)
    exchange_matrix = summed / math.sqrt(rows_dev * n_grid)
    return (terms, exchange_matrix)


def solution(mesh):
    in_specs = (P("grid", "orb"), P(), P("grid", ("orb", "pts")), P(("orb", "pts"), "grid"))
    out_specs = (P(("orb", "pts"), "grid"), P(("orb", "pts"), "grid"))
    return jax.shard_map(
        per_device, mesh=mesh, in_specs=in_specs, out_specs=out_specs, check_vma=False
    )
```

profile of v0, /device:TPU:0, one launch (start us, length us, event | category | flops | bytes accessed | tf_op | source)
XLA Modules:
  0.0 927.6 jit_solution(6591598182595387034)
XLA Ops:
  7.2 0.0 copy-start
  7.2 0.0 all-reduce.3.cloned.1.call-start
  7.2 0.8 compare_and_fusion.1
  8.1 0.8 fusion.11
  8.8 34.9 %gather_fusion = bf16[8192,512]{1,0:T(8,128)(2,1)} fusion(bf16[256,512]{1,0:T(8,128)(2,1)} %param.4, s32[8192]{0:T(1024)S(1)} %fusion.11), kind=kCustom, calls=%fused_computation | custom fusion | bytes 16809984 | tf_op jit(solution)/shard_map/jit(_take)/gather | solution.py:23
  43.8 8.5 select_convert_fusion
  52.3 0.0 all-reduce.3.cloned.1.call-update
  52.3 0.0 all-gather.6.cloned.1.call-start
  52.4 293.7 %all-reduce.3.cloned.1.call-done = bf16[8192,512]{1,0:T(8,128)(2,1)} async-done(((bf16[8192,512]{1,0:T(8,128)(2,1)}), bf16[8192,512]{1,0:T(8,128)(2,1)}) %all-reduce.3.cloned.1.call-update) | async-done | bytes 8388624 | tf_op jit(solution)/shard_map/psum | solution.py:25
  346.0 3.0 constant_dynamic-slice_fusion
  349.1 0.0 all-gather.6.cloned.1.call-update
  349.1 0.0 all-gather.4.cloned.1.call-start
  349.2 4.4 constant_dynamic-slice_fusion.1
  353.6 0.0 all-gather.4.cloned.1.call-update
  353.6 0.0 all-gather.8.cloned.1.call-start
  353.7 0.5 all-gather.8.cloned.1.call-update
  354.2 0.0 reduce-scatter.3.cloned.1.call-start
  354.2 52.3 %all-gather.6.cloned.1.call-done = bf16[2048,2048]{1,0:T(8,128)(2,1)} async-done(((bf16[2048,512]{1,0:T(8,128)(2,1)}), bf16[2048,2048]{1,0:T(8,128)(2,1)}) %all-gather.6.cloned.1.call-update) | async-done | bytes 8388624 | tf_op jit(solution)/shard_map/all_gather | solution.py:33
  406.5 107.5 %all-gather.4.cloned.1.call-done = bf16[4096,2048]{1,0:T(8,128)(2,1)} async-done(((bf16[4096,512]{1,0:T(8,128)(2,1)}), bf16[4096,2048]{1,0:T(8,128)(2,1)}) %all-gather.4.cloned.1.call-update) | async-done | bytes 16777232 | tf_op jit(solution)/shard_map/all_gather | solution.py:32
  514.0 27.6 %fusion.4 = f32[1024,2048]{1,0:T(8,128)} fusion(bf16[2048,2048]{1,0:T(8,128)(2,1)} %all-gather.6.cloned.1.call-done, bf16[1024,2048]{1,0:T(8,128)(2,1)} %param.7, bf16[4096,2048]{1,0:T(8,128)(2,1)} %all-gather.4.cloned.1.call-done, s32[]{:T(128)S(6)} %select_n.27), kind=kOutput, calls=%fused_computation.6 | convolution fusion | flops 17186160640 | bytes 33554436 | tf_op jit(solution)/shard_map/dot_general | solution.py:40
  541.6 286.5 %all-reduce.4 = bf16[1024,2048]{1,0:T(8,128)(2,1)} all-reduce(f32[1024,2048]{1,0:T(8,128)} %fusion.4), channel_id=1, replica_groups=mesh['grid'=4,'orb'=4,'pts'=2] {'grid'}, use_global_device_ids=true, to_apply=%region_1.2 | all-reduce | flops 2097152 | bytes 12582912 | tf_op jit(solution)/shard_map/psum | solution.py:41
  828.1 0.0 copy-done
  828.1 4.8 fusion.6
  833.0 0.0 reduce-scatter.3.cloned.1.call-update
  833.0 0.0 reduce-scatter.5.cloned.1.call-start
  833.0 0.0 all-gather.8.cloned.1.call-done
  833.1 38.9 %reduce-scatter.3.cloned.1.call-done = f32[256,256]{1,0:T(8,128)} async-done(((f32[2048,256]{1,0:T(8,128)}), f32[256,256]{1,0:T(8,128)}) %reduce-scatter.3.cloned.1.call-update) | async-done | bytes 262160 | tf_op jit(solution)/shard_map/reduce_scatter | solution.py:42
  872.0 3.1 fusion.9
  875.1 0.0 reduce-scatter.5.cloned.1.call-update
  875.1 43.8 %reduce-scatter.5.cloned.1.call-done = f32[256,512]{1,0:T(8,128)} async-done(((f32[256,2048]{1,0:T(8,128)}), f32[256,512]{1,0:T(8,128)}) %reduce-scatter.5.cloned.1.call-update) | async-done | bytes 524304 | tf_op jit(solution)/shard_map/reduce_scatter | solution.py:56
  918.9 1.9 broadcast_multiply_fusion
Async XLA Ops:
  7.2 821.0 %copy-start = (bf16[256,1024]{1,0:T(8,128)(2,1)S(1)}, bf16[256,1024]{1,0:T(8,128)(2,1)}, u32[]{:S(2)}) copy-start(bf16[256,1024]{1,0:T(8,128)(2,1)} %param.6) | copy-start | bytes 1572868
  7.2 338.9 %all-reduce.3.cloned.1.call-start = ((), (), s32[]{:S(2)}) async-start(), calls=%async_computation.2 | async-start | bytes 16777216 | tf_op jit(solution)/shard_map/psum | solution.py:25
  52.3 354.2 %all-gather.6.cloned.1.call-start = ((), (), s32[]{:S(2)}) async-start(), calls=%async_computation.4 | async-start | bytes 10485760 | tf_op jit(solution)/shard_map/all_gather | solution.py:33
  349.1 164.9 %all-gather.4.cloned.1.call-start = ((), (), s32[]{:S(2)}) async-start(), calls=%async_computation.3 | async-start | bytes 20971520 | tf_op jit(solution)/shard_map/all_gather | solution.py:32
  353.6 479.4 %all-gather.8.cloned.1.call-start = ((), (), s32[]{:S(2)}) async-start(), calls=%async_computation.6 | async-start | bytes 1310720 | tf_op jit(solution)/shard_map/all_gather | solution.py:53
  354.2 517.8 %reduce-scatter.3.cloned.1.call-start = ((), (), s32[]{:S(2)}) async-start(), calls=%async_computation.5 | async-start | bytes 2359296 | tf_op jit(solution)/shard_map/reduce_scatter | solution.py:42
  833.0 85.9 %reduce-scatter.5.cloned.1.call-start = ((), (), s32[]{:S(2)}) async-start(), calls=%async_computation.7 | async-start | bytes 2621440 | tf_op jit(solution)/shard_map/reduce_scatter | solution.py:56
Sparse Core Ops, SparseCore 0:
  52.5 293.5 all-reduce.2
  349.2 57.2 all-gather.5
  408.1 105.8 all-gather.3
  515.4 16.6 all-gather.7
  833.1 38.8 reduce-scatter.2
  875.2 43.5 reduce-scatter.4
where the time goes:
time: 928 us
  waiting for transfers between devices  537 us (58%)
  blocking collectives  287 us (31%)
  local copies, waits for them, and re-layouts  42.4 us (5%)
  matrix products  35.5 us (4%)
  between operations  14.2 us (2%)
  other arithmetic  12 us (1%)
    psum x1, waiting for transfers between devices, per_device(): picked = lax.psum(selected.astype(jnp.bfloat16), 'grid')  294 us
    psum x1, blocking collectives, per_device(): applied = lax.psum(partial_applied, 'grid').astype(jnp.bfloat16)  287 us
    all_gather x1, waiting for transfers between devices, per_device(): lax.all_gather(own_rows, 'orb', axis=1, tiled=True)  107 us
    all_gather x1, waiting for transfers between devices, per_device(): lax.all_gather(point_rows, 'orb', axis=1, tiled=True)  52.3 us
    reduce_scatter x1, waiting for transfers between devices, per_device(): lax.psum_scatter(partial_matrix, 'grid', scatter_dimension=1, tiled=True)  43.8 us
    reduce_scatter x1, waiting for transfers between devices, per_device(): lax.psum_scatter(-lax.dot_general(applied, fitting, (((0,), (1,)), ((), (...  38.9 us
    gather x1, local copies, waits for them, and re-layouts, per_device(): taken = jnp.take(orbitals, clamped, axis=0).astype(jnp.float32)  34.9 us
    dot_general x1, matrix products, per_device(): jnp.dot(masked, point_full, preferred_element_type=jnp.float32)  27.6 us
  transfers between devices with their start and end apart: 6, of which 5 were waited for; matrix products, arithmetic and copies ran while one was open for 4% of the time, Pallas kernels for 0%

commit v1 on v0

v1 whole, which is shorter than its diff:
```python
import math

import jax
import jax.numpy as jnp
from jax import lax
from jax.experimental import pallas as pl
from jax.experimental.pallas import tpu as pltpu
from jax.sharding import PartitionSpec as P

F32, BF16 = jnp.float32, jnp.bfloat16


def dot(a, b, ca, cb):
    return lax.dot_general(a, b, (((ca,), (cb,)), ((), ())), preferred_element_type=F32)


def middle(orb_ref, prow_ref, pcol_ref, fit_ref, scr_ref, v_ref, gram, rows, total):
    nrows = orb_ref.shape[0]
    npoint, ncol = scr_ref.shape
    tile = min(512, ncol)
    gtile = min(512, nrows)

    @pl.loop(0, nrows // gtile)
    def _(k):
        at = pl.ds(pl.multiple_of(k * gtile, gtile), gtile)
        gram[:, at] = dot(orb_ref[...], orb_ref[at, :], 1, 1).astype(BF16)

    hot = (lax.broadcasted_iota(jnp.int32, (npoint, nrows), 1) == prow_ref[...]).astype(F32)
    hot = hot.astype(BF16)

    @pl.loop(0, nrows // gtile)
    def _(k):
        at = pl.ds(pl.multiple_of(k * gtile, gtile), gtile)
        rows[:, at] = dot(hot, gram[:, at], 1, 0).astype(BF16)

    total[...] = jnp.zeros_like(total)

    @pl.loop(0, ncol // tile)
    def _(k):
        at = pl.ds(pl.multiple_of(k * tile, tile), tile)
        names = pcol_ref[:, at]
        pick = (lax.broadcasted_iota(jnp.int32, (nrows, tile), 0) == names).astype(F32).astype(BF16)
        density = dot(rows[...], pick, 1, 0)
        masked = (density * scr_ref[:, at].astype(F32)).astype(BF16)
        total[...] += dot(masked, pick, 1, 1)

    rows[...] = total[...].astype(BF16)

    @pl.loop(0, nrows // gtile)
    def _(k):
        at = pl.ds(pl.multiple_of(k * gtile, gtile), gtile)
        v_ref[:, at] = dot(fit_ref[...], rows[:, at], 1, 0)


def per_device(orbitals, points, fitting, screened):
    grid_index = lax.axis_index("grid")
    orb_index = lax.axis_index("orb")
    pts_index = lax.axis_index("pts")
    n_grid = lax.axis_size("grid")
    n_orb = lax.axis_size("orb")
    n_pts = lax.axis_size("pts")
    nrows = orbitals.shape[0] * n_grid
    width = orbitals.shape[1] * n_orb
    npoint, ncol = screened.shape
    block = orb_index * n_pts + pts_index
    full = lax.all_gather(
        lax.all_gather(orbitals, "orb", axis=1, tiled=True), "grid", axis=0, tiled=True
    )
    fit = lax.all_gather(fitting, "grid", axis=0, tiled=True)
    prow = lax.dynamic_slice_in_dim(points, block * npoint, npoint).reshape(npoint, 1)
    pcol = lax.dynamic_slice_in_dim(points, grid_index * ncol, ncol).reshape(1, ncol)
    v = pl.pallas_call(
        middle,
        out_shape=jax.ShapeDtypeStruct((nrows, nrows), F32),
        in_specs=[pl.BlockSpec(memory_space=pltpu.VMEM)] * 5,
        out_specs=pl.BlockSpec(memory_space=pltpu.VMEM),
        scratch_shapes=[
            pltpu.VMEM((nrows, nrows), BF16),
            pltpu.VMEM((npoint, nrows), BF16),
            pltpu.VMEM((npoint, nrows), F32),
        ],
        compiler_params=pltpu.CompilerParams(vmem_limit_bytes=60 * 2**20),
    )(full, prow, pcol, fit, screened)
    v = lax.psum_scatter(v, ("orb", "pts"), scatter_dimension=1, tiled=True)
    v = lax.psum_scatter(v, "grid", scatter_dimension=0, tiled=True).astype(BF16)
    v = lax.all_gather(v, ("orb", "pts"), axis=1, tiled=True)
    own = width // (n_orb * n_pts)
    mine = lax.dynamic_slice_in_dim(full, block * own, own, 1)
    terms = -dot(mine, v, 0, 1)
    rounded = lax.all_gather(terms.astype(BF16), "grid", axis=1, tiled=True)
    out_width = width // n_grid
    side = lax.dynamic_slice_in_dim(full, grid_index * out_width, out_width, 1)
    exchange_matrix = dot(rounded, side, 1, 0) / math.sqrt(nrows)
    return (terms, exchange_matrix)


def solution(mesh):
    in_specs = (P("grid", "orb"), P(), P("grid", ("orb", "pts")), P(("orb", "pts"), "grid"))
    out_specs = (P(("orb", "pts"), "grid"), P(("orb", "pts"), "grid"))
    return jax.shard_map(
        per_device, mesh=mesh, in_specs=in_specs, out_specs=out_specs, check_vma=False
    )
```

time: 928 us -> 304 us (0.33)
  waiting for transfers between devices: 537 us -> 221 us
  blocking collectives: 287 us -> 34.3 us
  local copies, waits for them, and re-layouts: 42.4 us -> 3.01 us
  matrix products: 35.5 us -> 4.56 us
  Pallas kernels: 0 us -> 26.4 us
  other arithmetic: 12 us -> 0.91 us
    psum x1 -> x0, waiting for transfers between devices: 294 us -> none  [per_device(): picked = lax.psum(selected.astype(jnp.bfloat16), 'grid')]
    psum x1 -> x0, blocking collectives: 287 us -> none  [per_device(): applied = lax.psum(partial_applied, 'grid').astype(jnp.bfloat16)]
    gather x1 -> x0, local copies, waits for them, and re-layouts: 34.9 us -> none  [per_device(): taken = jnp.take(orbitals, clamped, axis=0).astype(jnp.float32)]
    all_gather x2, waiting for transfers between devices: 160 us -> 125 us  [the longest x1 81.2 us: per_device(): lax.all_gather(lax.all_gather(orbitals, 'orb', axis=1, tiled=True), 'grid...]
    all_gather x0 -> x2, blocking collectives: none -> 34.3 us  [the longest x1 18.2 us: per_device(): v = lax.all_gather(v, ('orb', 'pts'), axis=1, tiled=True)]
    dot_general x3 -> x2, matrix products: 35.5 us -> 4.56 us  [dot(): lax.dot_general(a, b, (((ca,), (cb,)), ((), ())), preferred_element_type=...]
    pallas_call x0 -> x1, Pallas kernels: none -> 26.4 us  [per_device(): pl.pallas_call(middle, out_shape=jax.ShapeDtypeStruct((nrows, nrows), F32...]
    all_gather x1, waiting for transfers between devices: 0.02 us -> 20.3 us  [per_device(): lax.all_gather(orbitals, 'orb', axis=1, tiled=True)]
  transfers between devices with their start and end apart: 6 -> 5, of which waited for: 5 -> 5; matrix products, arithmetic and copies ran while one was open for 4% -> 1% of each run, Pallas kernels for 0% -> 0%
where the time goes in v1:
time: 304 us
  waiting for transfers between devices  221 us (73%)
  blocking collectives  34.3 us (11%)
  Pallas kernels  26.4 us (9%)
  between operations  13.8 us (5%)
  matrix products  4.56 us (1%)
    all_gather x1, waiting for transfers between devices, per_device(): lax.all_gather(lax.all_gather(orbitals, 'orb', axis=1, tiled=True), 'grid...  81.2 us
    reduce_scatter x1, waiting for transfers between devices, per_device(): v = lax.psum_scatter(v, ('orb', 'pts'), scatter_dimension=1, tiled=True)  49.6 us
    all_gather x1, waiting for transfers between devices, per_device(): fit = lax.all_gather(fitting, 'grid', axis=0, tiled=True)  44.2 us
    pallas_call x1, Pallas kernels, per_device(): pl.pallas_call(middle, out_shape=jax.ShapeDtypeStruct((nrows, nrows), F32...  26.4 us
    reduce_scatter x1, waiting for transfers between devices, per_device(): lax.psum_scatter(v, 'grid', scatter_dimension=0, tiled=True).astype(BF16)  23.9 us
    all_gather x1, waiting for transfers between devices, per_device(): lax.all_gather(orbitals, 'orb', axis=1, tiled=True)  20.3 us
    all_gather x1, blocking collectives, per_device(): v = lax.all_gather(v, ('orb', 'pts'), axis=1, tiled=True)  18.2 us
    all_gather x1, blocking collectives, per_device(): rounded = lax.all_gather(terms.astype(BF16), 'grid', axis=1, tiled=True)  16.1 us
  transfers between devices with their start and end apart: 5, of which 5 were waited for; matrix products, arithmetic and copies ran while one was open for 1% of the time, Pallas kernels for 0%

profile of v1, /device:TPU:0, one launch (start us, length us, event | category | flops | bytes accessed | tf_op | source)
XLA Modules:
  0.0 303.8 jit_solution(2491068865589023942)
XLA Ops:
  7.2 0.0 all-gather.4.cloned.1.call-start
  7.2 0.7 all-gather.4.cloned.1.call-update
  7.9 0.0 all-gather.8.cloned.1.call-start
  7.9 0.7 all-gather.8.cloned.1.call-update
  8.6 0.0 all-gather.6.cloned.1.call-start
  8.7 20.3 %all-gather.4.cloned.1.call-done = bf16[256,2048]{1,0:T(8,128)(2,1)} async-done(((bf16[256,512]{1,0:T(8,128)(2,1)}), bf16[256,2048]{1,0:T(8,128)(2,1)}) %all-gather.4.cloned.1.call-update) | async-done | bytes 1048592 | tf_op jit(solution)/shard_map/all_gather | solution.py:67
  29.0 0.0 all-gather.6.cloned.1.call-update
  29.0 0.0 reduce-scatter.3.cloned.1.call-start
  29.1 0.7 dynamic_slice.13
  29.8 1.3 dynamic_slice.14
  31.1 1.0 copy.6.prow_ref
  32.1 44.2 %all-gather.8.cloned.1.call-done.fit_ref = bf16[1024,1024]{1,0:T(8,128)(2,1)} async-done(((bf16[256,1024]{1,0:T(8,128)(2,1)}), bf16[1024,1024]{1,0:T(8,128)(2,1)}) %all-gather.8.cloned.1.call-update) | async-done | bytes 2097168 | tf_op jit(solution)/shard_map/all_gather | solution.py:69
  76.2 81.2 %all-gather.6.cloned.1.call-done.orb_ref = bf16[1024,2048]{1,0:T(8,128)(2,1)} async-done(((bf16[256,2048]{1,0:T(8,128)(2,1)}), bf16[1024,2048]{1,0:T(8,128)(2,1)}) %all-gather.6.cloned.1.call-update) | async-done | bytes 4194320 | tf_op jit(solution)/shard_map/all_gather | solution.py:66
  157.4 26.4 %shard_map.59 = f32[1024,1024]{1,0:T(8,128)} custom-call(bf16[1024,2048]{1,0:T(8,128)(2,1)} %all-gather.6.cloned.1.call-done.orb_ref, s32[1024,1]{1,0:T(8,128)} %copy.6.prow_ref, s32[1,2048]{1,0:T(1,128)} %bitcast.4, bf16[1024,1024]{1,0:T(8,128)(2,1)} %all-gather.8.cloned.1.call-done.fit_ref, bf16[1024,2048]{1,0:T(8,128)(2,1)} %scr_ref.1), custom_call_target="tpu_custom_call" | custom-call | tf_op jit(solution)/shard_map/pallas_call | solution.py:72
  183.8 0.0 reduce-scatter.3.cloned.1.call-update
  183.8 0.0 reduce-scatter.5.cloned.1.call-start
  183.8 49.6 %reduce-scatter.3.cloned.1.call-done = f32[1024,128]{1,0:T(8,128)} async-done(((f32[1024,1024]{1,0:T(8,128)}), f32[1024,128]{1,0:T(8,128)}) %reduce-scatter.3.cloned.1.call-update) | async-done | bytes 524304 | tf_op jit(solution)/shard_map/reduce_scatter | solution.py:84
  233.5 0.0 reduce-scatter.5.cloned.1.call-update
  233.5 23.9 %reduce-scatter.5.cloned.1.call-done = f32[256,128]{1,0:T(8,128)} async-done(((f32[1024,128]{1,0:T(8,128)}), f32[256,128]{1,0:T(8,128)}) %reduce-scatter.5.cloned.1.call-update) | async-done | bytes 131088 | tf_op jit(solution)/shard_map/reduce_scatter | solution.py:85
  257.4 0.9 convert_element_type.6
  258.4 18.2 %all_gather.18 = bf16[256,1024]{1,0:T(8,128)(2,1)S(1)} all-gather(bf16[256,128]{1,0:T(8,128)(2,1)S(1)} %convert_element_type.6), channel_id=1, replica_groups=mesh['grid'=4,'orb'=4,'pts'=2] {'orb','pts'}, dimensions={1}, use_global_device_ids=true | all-gather | bytes 589824 | tf_op jit(solution)/shard_map/all_gather | solution.py:86
  276.6 2.1 fusion.4
  278.7 16.1 %all_gather.19 = bf16[256,1024]{1,0:T(8,128)(2,1)S(1)} all-gather(bf16[256,256]{1,0:T(8,128)(2,1)S(1)} %get-tuple-element.2), channel_id=1, replica_groups=mesh['grid'=4,'orb'=4,'pts'=2] {'grid'}, dimensions={1}, use_global_device_ids=true | all-gather | bytes 655360 | tf_op jit(solution)/shard_map/all_gather | solution.py:90
  294.8 2.5 convolution_multiply_fusion
Async XLA Ops:
  7.2 21.8 %all-gather.4.cloned.1.call-start = ((), (), s32[]{:S(2)}) async-start(), calls=%async_computation.2 | async-start | bytes 1310720 | tf_op jit(solution)/shard_map/all_gather | solution.py:67
  7.9 68.3 %all-gather.8.cloned.1.call-start = ((), (), s32[]{:S(2)}) async-start(), calls=%async_computation.4 | async-start | bytes 2621440 | tf_op jit(solution)/shard_map/all_gather | solution.py:69
  8.6 148.8 %all-gather.6.cloned.1.call-start = ((), (), s32[]{:S(2)}) async-start(), calls=%async_computation.3 | async-start | bytes 5242880 | tf_op jit(solution)/shard_map/all_gather | solution.py:66
  29.0 204.5 %reduce-scatter.3.cloned.1.call-start = ((), (), s32[]{:S(2)}) async-start(), calls=%async_computation.5 | async-start | bytes 4718592 | tf_op jit(solution)/shard_map/reduce_scatter | solution.py:84
  183.8 73.6 %reduce-scatter.5.cloned.1.call-start = ((), (), s32[]{:S(2)}) async-start(), calls=%async_computation.6 | async-start | bytes 655360 | tf_op jit(solution)/shard_map/reduce_scatter | solution.py:85
Sparse Core Ops, SparseCore 0:
  9.5 19.4 all-gather.3
  30.6 45.6 all-gather.7
  77.8 79.5 all-gather.5
  183.9 49.5 reduce-scatter.2
  235.6 21.7 reduce-scatter.4

commit v2 on v1

v2 whole, which is shorter than its diff:
```python
import functools
import math

import jax
import jax.numpy as jnp
from jax import lax
from jax.experimental import pallas as pl
from jax.experimental.pallas import tpu as pltpu
from jax.sharding import PartitionSpec as P

F32, BF16 = jnp.float32, jnp.bfloat16
MESH = pl.DeviceIdType.MESH


def dot(a, b, ca, cb):
    return lax.dot_general(a, b, (((ca,), (cb,)), ((), ())), preferred_element_type=F32)


def span(start, size):
    return pl.ds(pl.multiple_of(start, size), size)


class Place:
    def __init__(self, sizes):
        self.nz, self.no, self.nx = sizes
        self.z = lax.axis_index("grid")
        self.o = lax.axis_index("orb")
        self.x = lax.axis_index("pts")
        self.core = lax.rem(self.o, 2)
        self.mate = self.o + 1 - 2 * self.core
        self.chips = (self.no // 2) * self.nx
        self.chip = (self.o // 2) * self.nx + self.x

    def other(self, j):
        c = lax.rem(self.chip + j, self.chips)
        return c, (c // self.nx) * 2 + self.core, lax.rem(c, self.nx)

    def at_mate(self):
        return {"orb": self.mate}


class Copies:
    def __init__(self):
        self.started = []

    def start(self, src, dst, send, recv, to, when=None):
        copy = pltpu.make_async_remote_copy(
            src_ref=src, dst_ref=dst, send_sem=send, recv_sem=recv, device_id=to, device_id_type=MESH
        )
        if when is None:
            copy.start()
        else:
            pl.when(when)(copy.start)
        self.started.append((copy, when))

    def finish(self):
        for copy, when in self.started:
            if when is None:
                copy.wait_send()
            else:
                pl.when(when)(copy.wait_send)


def arrived(dst, send, recv, to, when=None):
    copy = pltpu.make_async_remote_copy(
        src_ref=dst, dst_ref=dst, send_sem=send, recv_sem=recv, device_id=to, device_id_type=MESH
    )
    if when is None:
        copy.wait_recv()
    else:
        pl.when(when)(copy.wait_recv)


def first(sizes, orb_ref, prow_ref, pcol_ref, fit_ref, scr_ref, v_ref, mine_ref, side_ref,
          full, fit, gram, low, rows, rows_low, total, local_sem,
          o_recv, f_recv, right_sem, left_sem, plane_sem, mate_sem, f_right, f_left):
    me = Place(sizes)
    nz, chips, z = me.nz, me.chips, me.z
    deep, wide = orb_ref.shape
    half = deep // me.nx
    fdeep = fit_ref.shape[0]

    barrier = pltpu.get_barrier_semaphore()

    def greet(to):
        pl.semaphore_signal(barrier, inc=1, device_id=to, device_id_type=MESH)

    has_right, has_left = z < nz - 1, z > 0
    pl.when(has_right)(lambda: greet({"grid": z + 1}))
    pl.when(has_left)(lambda: greet({"grid": z - 1}))
    greet(me.at_mate())
    for j in range(1, chips):
        _, o, x = me.other(j)
        greet({"orb": o, "pts": x})
    pl.semaphore_wait(barrier, chips + has_right.astype(jnp.int32) + has_left.astype(jnp.int32))

    copies = Copies()

    def spot(zz, o, x):
        return full.at[span(zz * deep + x * half, half), span(o * wide, wide)]

    own_half = orb_ref.at[span(me.x * half, half), :]
    own_local = pltpu.make_async_copy(own_half, spot(z, me.o, me.x), local_sem.at[0])
    own_local.start()
    fit_local = pltpu.make_async_copy(fit_ref, fit.at[span(z * fdeep, fdeep), :], local_sem.at[1])
    fit_local.start()

    def plane(zz, src, s, when):
        for j in range(1, chips):
            _, o, x = me.other(j)
            copies.start(src, spot(zz, me.o, me.x), plane_sem.at[s, j], o_recv.at[zz, me.o, me.x],
                         {"orb": o, "pts": x}, when)

    def wait_piece(zz, o, x, when=None):
        arrived(spot(zz, o, x), local_sem.at[2], o_recv.at[zz, o, x], me.at_mate(), when)

    sides = []
    here = spot(z, me.o, me.x)
    copies.start(own_half, here, right_sem.at[0], o_recv.at[z, me.o, me.x], {"grid": z + 1}, has_right)
    copies.start(own_half, here, left_sem.at[0], o_recv.at[z, me.o, me.x], {"grid": z - 1}, has_left)
    plane(z, own_half, 0, None)
    for s in range(1, nz):
        lo, hi = jnp.maximum(z - s, 0), jnp.minimum(z + s, nz - 1)
        in_lo, in_hi = z - s >= 0, z + s < nz
        for zz, here_too, sem, to, onward in (
            (lo, in_lo, right_sem, z + 1, has_right), (hi, in_hi, left_sem, z - 1, has_left)
        ):
            wait_piece(zz, me.o, me.x, here_too)
            src = spot(zz, me.o, me.x)
            copies.start(src, src, sem.at[s], o_recv.at[zz, me.o, me.x], {"grid": to},
                         here_too & onward)
        plane(lo, spot(lo, me.o, me.x), 2 * s - 1, in_lo)
        plane(hi, spot(hi, me.o, me.x), 2 * s, in_hi)

    fit_here = fit.at[span(z * fdeep, fdeep), :]
    copies.start(fit_ref, fit_here, f_right.at[0], f_recv.at[z], {"grid": z + 1}, has_right)
    copies.start(fit_ref, fit_here, f_left.at[0], f_recv.at[z], {"grid": z - 1}, has_left)

    def pass_fit(s):
        for zz, here_too, sem, to, onward in (
            (jnp.maximum(z - s, 0), z - s >= 0, f_right, z + 1, has_right),
            (jnp.minimum(z + s, nz - 1), z + s < nz, f_left, z - 1, has_left),
        ):
            src = fit.at[span(zz * fdeep, fdeep), :]
            arrived(src, local_sem.at[2], f_recv.at[zz], me.at_mate(), here_too)
            copies.start(src, src, sem.at[s], f_recv.at[zz], {"grid": to}, here_too & onward)

    own_local.wait()
    for d in range(nz):
        zz = lax.rem(z + d, nz)
        for j in range(chips):
            _, o, x = me.other(j)
            if j > 0:
                wait_piece(zz, o, x)
            src = spot(zz, o, x)
            copies.start(src, src, mate_sem.at[d, j], o_recv.at[zz, o, x], me.at_mate())
    for d in range(nz):
        zz = lax.rem(z + d, nz)
        for j in range(chips):
            _, o, x = me.other(j)
            wait_piece(zz, o + 1 - 2 * me.core, x)

    if nz > 1:
        pass_fit(1)

    nrows = full.shape[0]
    npoint, ncol = scr_ref.shape
    tile = min(512, ncol)
    gtile = min(512, nrows)

    @pl.loop(0, nrows // gtile)
    def _(k):
        at = span(k * gtile, gtile)
        value = dot(full[...], full[at, :], 1, 1)
        rounded = value.astype(BF16)
        gram[:, at] = rounded
        low[:, at] = (value - rounded.astype(F32)).astype(BF16)

    hot = (lax.broadcasted_iota(jnp.int32, (npoint, nrows), 1) == prow_ref[...]).astype(F32)
    hot = hot.astype(BF16)

    @pl.loop(0, nrows // gtile)
    def _(k):
        at = span(k * gtile, gtile)
        rows[:, at] = dot(hot, gram[:, at], 1, 0).astype(BF16)
        rows_low[:, at] = dot(hot, low[:, at], 1, 0).astype(BF16)

    for s in range(2, nz):
        pass_fit(s)

    total[...] = jnp.zeros_like(total)

    @pl.loop(0, ncol // tile)
    def _(k):
        at = span(k * tile, tile)
        names = pcol_ref[:, at]
        pick = (lax.broadcasted_iota(jnp.int32, (nrows, tile), 0) == names).astype(F32).astype(BF16)
        density = dot(rows[...], pick, 1, 0) + dot(rows_low[...], pick, 1, 0)
        masked = (density * scr_ref[:, at].astype(F32)).astype(BF16)
        total[...] += dot(masked, pick, 1, 1)

    rows[...] = total[...].astype(BF16)
    own = mine_ref.shape[1]
    number = me.o * me.nx + me.x
    if own >= 128:
        mine_ref[...] = full[:, span(number * own, own)]
    else:
        parts = 128 // own
        block = full[:, span((number // parts) * 128, 128)]
        for k in range(parts):

            @pl.when(lax.rem(number, parts) == k)
            def _(k=k):
                mine_ref[...] = block[:, k * own : (k + 1) * own]

    own = side_ref.shape[1]
    side_ref[...] = full[:, span(z * own, own)]
    fit_local.wait()

    @pl.loop(0, nrows // gtile)
    def _(k):
        at = span(k * gtile, gtile)
        v_ref[:, at] = dot(fit[...], rows[:, at], 1, 0)

    copies.finish()


def second(sizes, v_ref, mine_ref, side_ref, terms_ref, matrix_ref,
           core_in, send, kept, plane_in, z_send, z_in, whole, rounded, dummy,
           core_s, core_r, plane_s, plane_r, z_s, z_r, w_s, w_r, m_s, e_s, e_r):
    me = Place(sizes)
    nz, chips, z = me.nz, me.chips, me.z
    nrows = v_ref.shape[0]
    deep = nrows // nz
    sub = deep // chips
    wide = nrows // 2

    barrier = pltpu.get_barrier_semaphore()

    def greet(to):
        pl.semaphore_signal(barrier, inc=1, device_id=to, device_id_type=MESH)

    greet(me.at_mate())
    for j in range(1, chips):
        _, o, x = me.other(j)
        greet({"orb": o, "pts": x})
    for d in range(1, nz):
        greet({"grid": lax.rem(z + d, nz)})
    pl.semaphore_wait(barrier, chips + nz - 1)

    copies = Copies()

    def got(dst, recv):
        arrived(dst, dummy.at[0], recv, me.at_mate())

    mine_cols, mate_cols = span(me.core * wide, wide), span((1 - me.core) * wide, wide)
    order = [(d, lax.rem(z + d, nz)) for d in range(1, nz + 1)]
    for d, zz in order:
        at = span(zz * deep, deep)
        copies.start(v_ref.at[at, mate_cols], core_in.at[at, :], core_s.at[d - 1], core_r.at[d - 1],
                     me.at_mate())
    for d, zz in order:
        at = span(zz * deep, deep)
        got(core_in.at[at, :], core_r.at[d - 1])
        for j in range(chips):
            c, o, x = me.other(j)
            part = span(zz * deep + c * sub, sub)
            value = v_ref[part, mine_cols] + core_in[part, :]
            if j == 0:
                kept[d - 1] = value
            else:
                send[d - 1, j - 1] = value.astype(BF16)
                copies.start(send.at[d - 1, j - 1], plane_in.at[d - 1, j - 1],
                             plane_s.at[d - 1, j - 1], plane_r.at[d - 1, j - 1], {"orb": o, "pts": x})
    for d, zz in order:
        value = kept[d - 1]
        for j in range(1, chips):
            got(plane_in.at[d - 1, j - 1], plane_r.at[d - 1, j - 1])
            value = value + plane_in[d - 1, j - 1].astype(F32)
        if d < nz:
            z_send[d - 1] = value.astype(BF16)
            copies.start(z_send.at[d - 1], z_in.at[d - 1], z_s.at[d - 1], z_r.at[d - 1], {"grid": zz})
    for d in range(1, nz):
        got(z_in.at[d - 1], z_r.at[d - 1])
        value = value + z_in[d - 1].astype(F32)

    def piece(c, core):
        return whole.at[span(c * sub, sub), span(core * wide, wide)]

    whole[span(me.chip * sub, sub), mine_cols] = value.astype(BF16)
    own_piece = piece(me.chip, me.core)
    for j in range(1, chips):
        _, o, x = me.other(j)
        copies.start(own_piece, own_piece, w_s.at[j - 1], w_r.at[me.chip, me.core], {"orb": o, "pts": x})
    for j in range(chips):
        c, _, _ = me.other(j)
        src = piece(c, me.core)
        if j > 0:
            got(src, w_r.at[c, me.core])
        copies.start(src, src, m_s.at[j], w_r.at[c, me.core], me.at_mate())
    for j in range(chips):
        c, _, _ = me.other(j)
        got(piece(c, 1 - me.core), w_r.at[c, 1 - me.core])

    exchange = -dot(mine_ref[...], whole[...], 0, 1)
    terms_ref[...] = exchange
    rounded[z] = exchange.astype(BF16)
    for d in range(1, nz):
        copies.start(rounded.at[z], rounded.at[z], e_s.at[d - 1], e_r.at[z],
                     {"grid": lax.rem(z + d, nz)})
    total = dot(rounded[z], side_ref[span(z * deep, deep), :], 1, 0)
    for d in range(1, nz):
        zz = lax.rem(z + d, nz)
        got(rounded.at[zz], e_r.at[zz])
        total = total + dot(rounded[zz], side_ref[span(zz * deep, deep), :], 1, 0)
    matrix_ref[...] = total / math.sqrt(nrows)
    copies.finish()


def per_device(orbitals, points, fitting, screened):
    grid_index = lax.axis_index("grid")
    block = lax.axis_index("orb") * lax.axis_size("pts") + lax.axis_index("pts")
    sizes = nz, no, nx = lax.axis_size("grid"), lax.axis_size("orb"), lax.axis_size("pts")
    nrows = orbitals.shape[0] * nz
    width = orbitals.shape[1] * no
    npoint, ncol = screened.shape
    chips = (no // 2) * nx
    prow = lax.dynamic_slice_in_dim(points, block * npoint, npoint).reshape(npoint, 1)
    pcol = lax.dynamic_slice_in_dim(points, grid_index * ncol, ncol).reshape(1, ncol)
    vmem = pl.BlockSpec(memory_space=pltpu.VMEM)
    dma = pltpu.SemaphoreType.DMA
    own, out_width = width // (no * nx), width // nz
    v, mine, side = pl.pallas_call(
        functools.partial(first, sizes),
        out_shape=(
            jax.ShapeDtypeStruct((nrows, nrows), F32),
            jax.ShapeDtypeStruct((nrows, own), BF16),
            jax.ShapeDtypeStruct((nrows, out_width), BF16),
        ),
        in_specs=[vmem] * 5,
        out_specs=(vmem,) * 3,
        scratch_shapes=[
            pltpu.VMEM((nrows, width), BF16),
            pltpu.VMEM((nrows, npoint), BF16),
            pltpu.VMEM((nrows, nrows), BF16),
            pltpu.VMEM((nrows, nrows), BF16),
            pltpu.VMEM((npoint, nrows), BF16),
            pltpu.VMEM((npoint, nrows), BF16),
            pltpu.VMEM((npoint, nrows), F32),
            dma((3,)),
            dma((nz, no, nx)),
            dma((nz,)),
            dma((nz,)),
            dma((nz,)),
            dma((2 * nz, chips)),
            dma((nz, chips)),
            dma((nz,)),
            dma((nz,)),
        ],
        compiler_params=pltpu.CompilerParams(
            collective_id=0, has_side_effects=True, vmem_limit_bytes=60 * 2**20
        ),
    )(orbitals, prow, pcol, fitting, screened)
    deep = nrows // nz
    sub, wide = deep // chips, nrows // 2
    others = max(chips - 1, 1)
    return pl.pallas_call(
        functools.partial(second, sizes),
        out_shape=(
            jax.ShapeDtypeStruct((own, deep), F32),
            jax.ShapeDtypeStruct((own, out_width), F32),
        ),
        in_specs=[vmem] * 3,
        out_specs=(vmem,) * 2,
        scratch_shapes=[
            pltpu.VMEM((nrows, wide), F32),
            pltpu.VMEM((nz, others, sub, wide), BF16),
            pltpu.VMEM((nz, sub, wide), F32),
            pltpu.VMEM((nz, others, sub, wide), BF16),
            pltpu.VMEM((nz, sub, wide), BF16),
            pltpu.VMEM((nz, sub, wide), BF16),
            pltpu.VMEM((deep, nrows), BF16),
            pltpu.VMEM((nz, own, deep), BF16),
            dma((1,)),
            dma((nz,)),
            dma((nz,)),
            dma((nz, others)),
            dma((nz, others)),
            dma((nz,)),
            dma((nz,)),
            dma((others,)),
            dma((chips, 2)),
            dma((chips,)),
            dma((nz,)),
            dma((nz,)),
        ],
        compiler_params=pltpu.CompilerParams(
            collective_id=1, has_side_effects=True, vmem_limit_bytes=60 * 2**20
        ),
    )(v, mine, side)


def solution(mesh):
    in_specs = (P("grid", "orb"), P(), P("grid", ("orb", "pts")), P(("orb", "pts"), "grid"))
    out_specs = (P(("orb", "pts"), "grid"), P(("orb", "pts"), "grid"))
    return jax.shard_map(
        per_device, mesh=mesh, in_specs=in_specs, out_specs=out_specs, check_vma=False
    )
```

time: 304 us -> 128 us (0.42)
  waiting for transfers between devices: 221 us -> 0 us
  Pallas kernels: 26.4 us -> 120 us
  blocking collectives: 34.3 us -> 0 us
  between operations: 13.8 us -> 0.66 us
  matrix products: 4.56 us -> 0 us
  local copies, waits for them, and re-layouts: 3.01 us -> 6.55 us
    all_gather x3 -> x0, waiting for transfers between devices: 146 us -> none  [the longest x1 81.2 us: per_device(): lax.all_gather(lax.all_gather(orbitals, 'orb', axis=1, tiled=True), 'grid...]
    pallas_call x1 -> x2, Pallas kernels: 26.4 us -> 120 us  [the longest x1 79.2 us: per_device(): pl.pallas_call(functools.partial(first, sizes), out_shape=(jax.ShapeDtype...]
    reduce_scatter x2 -> x0, waiting for transfers between devices: 73.6 us -> none  [the longest x1 49.6 us: per_device(): v = lax.psum_scatter(v, ('orb', 'pts'), scatter_dimension=1, tiled=True)]
    all_gather x2 -> x0, blocking collectives: 34.3 us -> none  [the longest x1 18.2 us: per_device(): v = lax.all_gather(v, ('orb', 'pts'), axis=1, tiled=True)]
    dot_general x2 -> x0, matrix products: 4.56 us -> none  [dot(): lax.dot_general(a, b, (((ca,), (cb,)), ((), ())), preferred_element_type=...]
    unnamed x0 -> x2, local copies, waits for them, and re-layouts: none -> 3.54 us
  transfers between devices with their start and end apart: 5 -> 0, of which waited for: 5 -> 0; matrix products, arithmetic and copies ran while one was open for 1% -> 0% of each run, Pallas kernels for 0% -> 0%
where the time goes in v2:
time: 128 us; the launch traced here: 127 us
  Pallas kernels  120 us (94%)
  local copies, waits for them, and re-layouts  6.55 us (5%)
    pallas_call x1, Pallas kernels, per_device(): pl.pallas_call(functools.partial(first, sizes), out_shape=(jax.ShapeDtype...  79.2 us
    pallas_call x1, Pallas kernels, per_device(): pl.pallas_call(functools.partial(second, sizes), out_shape=(jax.ShapeDtyp...  40.5 us
    unnamed x2, local copies, waits for them, and re-layouts  3.54 us

profile of v2, /device:TPU:0, one launch (start us, length us, event | category | flops | bytes accessed | tf_op | source)
XLA Modules:
  0.0 126.9 jit_solution(12602872904624828042)
XLA Ops:
  0.6 0.7 dynamic_slice.6
  1.3 1.3 %dynamic_slice.7 = s32[2048]{0:T(1024)} dynamic-slice(s32[8192]{0:T(1024)} %param.5, s32[]{:T(128)S(6)} %select_n.7), dynamic_slice_sizes={2048} | dynamic-slice | bytes 16388 | tf_op jit(solution)/shard_map/dynamic_slice | solution.py:329
  2.6 1.0 copy.6.prow_ref
  3.6 79.2 %shard_map.59 = (f32[1024,1024]{1,0:T(8,128)}, bf16[1024,256]{1,0:T(8,128)(2,1)}, bf16[1024,512]{1,0:T(8,128)(2,1)}) custom-call(bf16[256,512]{1,0:T(8,128)(2,1)} %orb_ref.1, s32[1024,1]{1,0:T(8,128)} %copy.6.prow_ref, s32[1,2048]{1,0:T(1,128)} %bitcast.2, bf16[256,1024]{1,0:T(8,128)(2,1)} %fit_ref.1, bf16[1024,2048]{1,0:T(8,128)(2,1)} %scr_ref.1), custom_call_target="tpu_custom_call" | custom-call | tf_op jit(solution)/shard_map/pallas_call | solution.py:333
  82.9 40.5 %shard_map.60 = (f32[256,256]{1,0:T(8,128)}, f32[256,512]{1,0:T(8,128)}) custom-call(f32[1024,1024]{1,0:T(8,128)} %get-tuple-element.5.v_ref, bf16[1024,256]{1,0:T(8,128)(2,1)} %get-tuple-element.6.mine_ref, bf16[1024,512]{1,0:T(8,128)(2,1)} %get-tuple-element.7.side_ref), custom_call_target="tpu_custom_call" | custom-call | tf_op jit(solution)/shard_map/pallas_call | solution.py:367
  123.4 1.7 %copy.9 = f32[256,256]{1,0:T(8,128)} copy(f32[256,256]{1,0:T(8,128)} %get-tuple-element.10) | data formatting | bytes 524288
  125.1 1.9 %copy.10 = f32[256,512]{1,0:T(8,128)} copy(f32[256,512]{1,0:T(8,128)} %get-tuple-element.11) | data formatting | bytes 1048576

commit v3 on v2

v3 whole, which is shorter than its diff:
```python
import functools
import math

import jax
import jax.numpy as jnp
from jax import lax
from jax.experimental import pallas as pl
from jax.experimental.pallas import tpu as pltpu
from jax.sharding import PartitionSpec as P

F32, BF16 = jnp.float32, jnp.bfloat16
MESH = pl.DeviceIdType.MESH


def dot(a, b, ca, cb):
    return lax.dot_general(a, b, (((ca,), (cb,)), ((), ())), preferred_element_type=F32)


def span(start, size):
    return pl.ds(pl.multiple_of(start, size), size)


class Place:
    def __init__(self, sizes):
        self.nz, self.no, self.nx = sizes
        self.z = lax.axis_index("grid")
        self.o = lax.axis_index("orb")
        self.x = lax.axis_index("pts")
        self.core = lax.rem(self.o, 2)
        self.mate = self.o + 1 - 2 * self.core
        self.chips = (self.no // 2) * self.nx
        self.chip = (self.o // 2) * self.nx + self.x

    def other(self, j):
        c = lax.rem(self.chip + j, self.chips)
        return c, (c // self.nx) * 2 + self.core, lax.rem(c, self.nx)

    def at_mate(self):
        return {"orb": self.mate}


class Copies:
    def __init__(self):
        self.started = []

    def start(self, src, dst, send, recv, to, when=None):
        copy = pltpu.make_async_remote_copy(
            src_ref=src, dst_ref=dst, send_sem=send, recv_sem=recv, device_id=to, device_id_type=MESH
        )
        if when is None:
            copy.start()
        else:
            pl.when(when)(copy.start)
        self.started.append((copy, when))

    def finish(self):
        for copy, when in self.started:
            if when is None:
                copy.wait_send()
            else:
                pl.when(when)(copy.wait_send)


def arrived(dst, send, recv, to, when=None):
    copy = pltpu.make_async_remote_copy(
        src_ref=dst, dst_ref=dst, send_sem=send, recv_sem=recv, device_id=to, device_id_type=MESH
    )
    if when is None:
        copy.wait_recv()
    else:
        pl.when(when)(copy.wait_recv)


def fused(sizes, orb_ref, points_ref, fit_ref, scr_ref, terms_ref, matrix_ref,
          full, fit, gram, low, rows, rows_low, total, mine, v_mate, v_own, core_in, send, plane_in,
          z_send, z_in, exchange, local_sem,
          o_recv, f_recv, right_sem, left_sem, plane_sem, mate_sem, f_sem,
          core_s, core_r, plane_s, plane_r, z_s, z_r, w_z, w_p, w_m, w_r):
    me = Place(sizes)
    nz, chips, z = me.nz, me.chips, me.z
    deep, wide = orb_ref.shape
    half = deep // me.nx

    barrier = pltpu.get_barrier_semaphore()

    def greet(to):
        pl.semaphore_signal(barrier, inc=1, device_id=to, device_id_type=MESH)

    greet(me.at_mate())
    for j in range(1, chips):
        _, o, x = me.other(j)
        greet({"orb": o, "pts": x})
    for d in range(1, nz):
        greet({"grid": lax.rem(z + d, nz)})
    pl.semaphore_wait(barrier, chips + nz - 1)

    has_right, has_left = z < nz - 1, z > 0
    copies = Copies()

    def got(dst, recv, when=None):
        arrived(dst, local_sem.at[2], recv, me.at_mate(), when)

    def spot(zz, o, x):
        return full.at[span(zz * deep + x * half, half), span(o * wide, wide)]

    own_half = orb_ref.at[span(me.x * half, half), :]
    own_local = pltpu.make_async_copy(own_half, spot(z, me.o, me.x), local_sem.at[0])
    own_local.start()
    fit_local = pltpu.make_async_copy(fit_ref, fit.at[span(z * deep, deep), :], local_sem.at[1])
    fit_local.start()

    def plane(zz, src, s, when):
        for j in range(1, chips):
            _, o, x = me.other(j)
            copies.start(src, spot(zz, me.o, me.x), plane_sem.at[s, j], o_recv.at[zz, me.o, me.x],
                         {"orb": o, "pts": x}, when)

    def wait_piece(zz, o, x, when=None):
        got(spot(zz, o, x), o_recv.at[zz, o, x], when)

    here = spot(z, me.o, me.x)
    copies.start(own_half, here, right_sem.at[0], o_recv.at[z, me.o, me.x], {"grid": z + 1}, has_right)
    copies.start(own_half, here, left_sem.at[0], o_recv.at[z, me.o, me.x], {"grid": z - 1}, has_left)
    plane(z, own_half, 0, None)
    for s in range(1, nz):
        lo, hi = jnp.maximum(z - s, 0), jnp.minimum(z + s, nz - 1)
        in_lo, in_hi = z - s >= 0, z + s < nz
        for zz, here_too, sem, to, onward in (
            (lo, in_lo, right_sem, z + 1, has_right), (hi, in_hi, left_sem, z - 1, has_left)
        ):
            wait_piece(zz, me.o, me.x, here_too)
            src = spot(zz, me.o, me.x)
            copies.start(src, src, sem.at[s], o_recv.at[zz, me.o, me.x], {"grid": to},
                         here_too & onward)
        plane(lo, spot(lo, me.o, me.x), 2 * s - 1, in_lo)
        plane(hi, spot(hi, me.o, me.x), 2 * s, in_hi)

    for d in range(1, nz):
        copies.start(fit_ref, fit.at[span(z * deep, deep), :], f_sem.at[d], f_recv.at[z],
                     {"grid": lax.rem(z + d, nz)})

    own_local.wait()
    for d in range(nz):
        zz = lax.rem(z + d, nz)
        for j in range(chips):
            _, o, x = me.other(j)
            if j > 0:
                wait_piece(zz, o, x)
            src = spot(zz, o, x)
            copies.start(src, src, mate_sem.at[d, j], o_recv.at[zz, o, x], me.at_mate())
    for d in range(nz):
        zz = lax.rem(z + d, nz)
        for j in range(chips):
            _, o, x = me.other(j)
            wait_piece(zz, o + 1 - 2 * me.core, x)

    nrows = full.shape[0]
    npoint, ncol = scr_ref.shape
    tile = min(512, ncol)
    gtile = min(512, nrows)
    number = me.o * me.nx + me.x

    @pl.loop(0, nrows // gtile)
    def _(k):
        at = span(k * gtile, gtile)
        value = dot(full[...], full[at, :], 1, 1)
        rounded = value.astype(BF16)
        gram[:, at] = rounded
        low[:, at] = (value - rounded.astype(F32)).astype(BF16)

    names = points_ref[:, span(number * npoint, npoint)].astype(F32)
    names = jnp.transpose(jnp.broadcast_to(names, (128, npoint)))[:, :1]
    hot = (lax.broadcasted_iota(jnp.int32, (npoint, nrows), 1) == names.astype(jnp.int32))
    hot = hot.astype(F32).astype(BF16)

    @pl.loop(0, nrows // gtile)
    def _(k):
        at = span(k * gtile, gtile)
        rows[:, at] = dot(hot, gram[:, at], 1, 0).astype(BF16)
        rows_low[:, at] = dot(hot, low[:, at], 1, 0).astype(BF16)

    total[...] = jnp.zeros_like(total)

    @pl.loop(0, ncol // tile)
    def _(k):
        at = span(k * tile, tile)
        names = points_ref[:, span(z * ncol + k * tile, tile)]
        pick = (lax.broadcasted_iota(jnp.int32, (nrows, tile), 0) == names).astype(F32).astype(BF16)
        density = dot(rows[...], pick, 1, 0) + dot(rows_low[...], pick, 1, 0)
        masked = (density * scr_ref[:, at].astype(F32)).astype(BF16)
        total[...] += dot(masked, pick, 1, 1)

    rows[...] = total[...].astype(BF16)
    own = mine.shape[1]
    if own >= 128:
        mine[...] = full[:, span(number * own, own)]
    else:
        parts = 128 // own
        block = full[:, span((number // parts) * 128, 128)]
        for k in range(parts):

            @pl.when(lax.rem(number, parts) == k)
            def _(k=k):
                mine[...] = block[:, k * own : (k + 1) * own]

    sub, wide = deep // chips, nrows // 2
    mine_cols, mate_cols = span(me.core * wide, wide), span((1 - me.core) * wide, wide)
    order = [(d, lax.rem(z + d, nz)) for d in range(1, nz + 1)]
    for d, zz in order:
        at = span(zz * deep, deep)
        if d < nz:
            got(fit.at[at, :], f_recv.at[zz])
        else:
            fit_local.wait()
        v_mate[d - 1] = dot(fit[at, :], rows[:, mate_cols], 1, 0).astype(BF16)
        copies.start(v_mate.at[d - 1], core_in.at[d - 1], core_s.at[d - 1], core_r.at[d - 1], me.at_mate())
        v_own[d - 1] = dot(fit[at, :], rows[:, mine_cols], 1, 0)
    for d, zz in order:
        got(core_in.at[d - 1], core_r.at[d - 1])
        for j in list(range(1, chips)) + [0]:
            c, o, x = me.other(j)
            part = span(c * sub, sub)
            value = v_own[d - 1, part, :] + core_in[d - 1, part, :].astype(F32)
            if j == 0:
                v_own[d - 1, part, :] = value
            else:
                send[d - 1, j - 1] = value.astype(BF16)
                copies.start(send.at[d - 1, j - 1], plane_in.at[d - 1, j - 1],
                             plane_s.at[d - 1, j - 1], plane_r.at[d - 1, j - 1], {"orb": o, "pts": x})
    for d, zz in order:
        value = v_own[d - 1, span(me.chip * sub, sub), :]
        for j in range(1, chips):
            got(plane_in.at[d - 1, j - 1], plane_r.at[d - 1, j - 1])
            value = value + plane_in[d - 1, j - 1].astype(F32)
        if d < nz:
            z_send[d - 1] = value.astype(BF16)
            copies.start(z_send.at[d - 1], z_in.at[d - 1], z_s.at[d - 1], z_r.at[d - 1], {"grid": zz})
    for d in range(1, nz):
        got(z_in.at[d - 1], z_r.at[d - 1])
        value = value + z_in[d - 1].astype(F32)

    def piece(zz, c, core):
        return gram.at[span(zz * deep + c * sub, sub), span(core * wide, wide)]

    def pass_on(zz, d, j):
        c, _, _ = me.other(j)
        src = piece(zz, c, me.core)
        copies.start(src, src, w_m.at[d, j], w_r.at[zz, c, me.core], me.at_mate())

    gram[span(z * deep + me.chip * sub, sub), mine_cols] = value.astype(BF16)
    own_piece = piece(z, me.chip, me.core)
    for d in range(1, nz):
        copies.start(own_piece, own_piece, w_z.at[d], w_r.at[z, me.chip, me.core],
                     {"grid": lax.rem(z + d, nz)})
    for d in range(nz):
        zz = lax.rem(z + d, nz)
        src = piece(zz, me.chip, me.core)
        if d > 0:
            got(src, w_r.at[zz, me.chip, me.core])
        for j in range(1, chips):
            _, o, x = me.other(j)
            copies.start(src, src, w_p.at[d, j], w_r.at[zz, me.chip, me.core], {"orb": o, "pts": x})
        pass_on(zz, d, 0)
    for d in range(nz):
        zz = lax.rem(z + d, nz)
        for j in range(1, chips):
            c, _, _ = me.other(j)
            got(piece(zz, c, me.core), w_r.at[zz, c, me.core])
            pass_on(zz, d, j)
    for d in range(nz):
        zz = lax.rem(z + d, nz)
        for j in range(chips):
            c, _, _ = me.other(j)
            got(piece(zz, c, 1 - me.core), w_r.at[zz, c, 1 - me.core])

    exchange[...] = -dot(mine[...], gram[...], 0, 1)
    terms_ref[...] = exchange[:, span(z * deep, deep)]
    out = matrix_ref.shape[1]
    matrix_ref[...] = dot(exchange[...].astype(BF16), full[:, span(z * out, out)], 1, 0)
    copies.finish()


def finish(nrows, terms_ref, matrix_ref, terms_out, matrix_out):
    terms_out[...] = terms_ref[...]
    matrix_out[...] = matrix_ref[...] / math.sqrt(nrows)


def per_device(orbitals, points, fitting, screened):
    sizes = nz, no, nx = lax.axis_size("grid"), lax.axis_size("orb"), lax.axis_size("pts")
    deep, columns = orbitals.shape
    nrows, width = deep * nz, columns * no
    npoint, ncol = screened.shape
    chips = (no // 2) * nx
    vmem = pl.BlockSpec(memory_space=pltpu.VMEM)
    dma = pltpu.SemaphoreType.DMA
    own, out_width = width // (no * nx), width // nz
    sub, wide = deep // chips, nrows // 2
    others = max(chips - 1, 1)
    outs = (
        jax.ShapeDtypeStruct((own, deep), F32),
        jax.ShapeDtypeStruct((own, out_width), F32),
    )
    results = pl.pallas_call(
        functools.partial(fused, sizes),
        out_shape=outs,
        in_specs=[vmem] * 4,
        out_specs=(vmem,) * 2,
        scratch_shapes=[
            pltpu.VMEM((nrows, width), BF16),
            pltpu.VMEM((nrows, npoint), BF16),
            pltpu.VMEM((nrows, nrows), BF16),
            pltpu.VMEM((nrows, nrows), BF16),
            pltpu.VMEM((npoint, nrows), BF16),
            pltpu.VMEM((npoint, nrows), BF16),
            pltpu.VMEM((npoint, nrows), F32),
            pltpu.VMEM((nrows, own), BF16),
            pltpu.VMEM((nz, deep, wide), BF16),
            pltpu.VMEM((nz, deep, wide), F32),
            pltpu.VMEM((nz, deep, wide), BF16),
            pltpu.VMEM((nz, others, sub, wide), BF16),
            pltpu.VMEM((nz, others, sub, wide), BF16),
            pltpu.VMEM((nz, sub, wide), BF16),
            pltpu.VMEM((nz, sub, wide), BF16),
            pltpu.VMEM((own, nrows), F32),
            dma((3,)),
            dma((nz, no, nx)),
            dma((nz,)),
            dma((nz,)),
            dma((nz,)),
            dma((2 * nz, chips)),
            dma((nz, chips)),
            dma((nz,)),
            dma((nz,)),
            dma((nz,)),
            dma((nz, others)),
            dma((nz, others)),
            dma((nz,)),
            dma((nz,)),
            dma((nz,)),
            dma((nz, chips)),
            dma((nz, chips)),
            dma((nz, chips, 2)),
        ],
        compiler_params=pltpu.CompilerParams(
            collective_id=0, has_side_effects=True, vmem_limit_bytes=63 * 2**20
        ),
    )(orbitals, points.reshape(1, -1), fitting, screened)
    return pl.pallas_call(
        functools.partial(finish, nrows),
        out_shape=outs,
        in_specs=[vmem] * 2,
        out_specs=(vmem,) * 2,
    )(*results)


def solution(mesh):
    in_specs = (P("grid", "orb"), P(), P("grid", ("orb", "pts")), P(("orb", "pts"), "grid"))
    out_specs = (P(("orb", "pts"), "grid"), P(("orb", "pts"), "grid"))
    return jax.shard_map(
        per_device, mesh=mesh, in_specs=in_specs, out_specs=out_specs, check_vma=False
    )
```

time: 128 us -> 106 us (0.83)
  the two profiles are of different devices: /device:TPU:0 before, /device:TPU:19 now
where the time goes in v3:
time: 106 us; the launch traced here: 105 us
  Pallas kernels  105 us (99%)
    pallas_call x1, Pallas kernels, per_device(): pl.pallas_call(functools.partial(fused, sizes), out_shape=outs, in_specs=...  103 us

profile of v3, /device:TPU:19, one launch (start us, length us, event | category | flops | bytes accessed | tf_op | source)
XLA Modules:
  0.0 105.5 jit_solution(12232328126851113102)
XLA Ops:
  0.6 102.8 %shard_map.59 = (f32[256,256]{1,0:T(8,128)}, f32[256,512]{1,0:T(8,128)}) custom-call(bf16[256,512]{1,0:T(8,128)(2,1)} %orb_ref.1, s32[1,8192]{1,0:T(1,128)} %bitcast.1, bf16[256,1024]{1,0:T(8,128)(2,1)} %fit_ref.1, bf16[1024,2048]{1,0:T(8,128)(2,1)} %scr_ref.1), custom_call_target="tpu_custom_call" | custom-call | tf_op jit(solution)/shard_map/pallas_call | solution.py:303
  103.4 2.1 %shard_map.60 = (f32[256,256]{1,0:T(8,128)}, f32[256,512]{1,0:T(8,128)}) custom-call(f32[256,256]{1,0:T(8,128)} %get-tuple-element.4.terms_ref, f32[256,512]{1,0:T(8,128)} %get-tuple-element.5.matrix_ref), custom_call_target="tpu_custom_call" | custom-call | tf_op jit(solution)/shard_map/pallas_call | solution.py:348

commit v4 on v3

--- a/solution.py
+++ b/solution.py
@@ -35,6 +35,23 @@
         c = lax.rem(self.chip + j, self.chips)
         return c, (c // self.nx) * 2 + self.core, lax.rem(c, self.nx)
 
+    def peer(self, ja, jx):
+        a = lax.rem(self.o // 2 + ja, self.no // 2)
+        x = lax.rem(self.x + jx, self.nx)
+        return a * self.nx + x, a * 2 + self.core, x
+
+    def peers(self):
+        near = [(0, jx) for jx in range(1, self.nx)] + [(ja, 0) for ja in range(1, self.no // 2)]
+        far = [(ja, jx) for ja in range(1, self.no // 2) for jx in range(1, self.nx)]
+        return near + far, []
+
+    def onward(self, d, ja, jx):
+        if False:
+            return [(k, jx, k, 0) for k in range(1, self.no // 2)]
+        if False:
+            return [(ja, k, 0, k) for k in range(1, self.nx)]
+        return []
+
     def at_mate(self):
         return {"orb": self.mate}
 
@@ -71,10 +88,10 @@
         pl.when(when)(copy.wait_recv)
 
 
-def fused(sizes, orb_ref, points_ref, fit_ref, scr_ref, terms_ref, matrix_ref,
-          full, fit, gram, low, rows, rows_low, total, mine, v_mate, v_own, core_in, send, plane_in,
+def fused(sizes, orb_ref, points_ref, fit_ref, scr_any, terms_ref, matrix_ref,
+          scr_ref, full, fit, gram, low, rows, rows_low, total, mine, v_mate, v_own, core_in, send, plane_in,
           z_send, z_in, exchange, local_sem,
-          o_recv, f_recv, right_sem, left_sem, plane_sem, mate_sem, f_sem,
+          o_recv, f_recv, right_sem, left_sem, plane_sem, mate_sem, f_sem, onward_sem, relay_sem,
           core_s, core_r, plane_s, plane_r, z_s, z_r, w_z, w_p, w_m, w_r):
     me = Place(sizes)
     nz, chips, z = me.nz, me.chips, me.z
@@ -96,6 +113,7 @@
 
     has_right, has_left = z < nz - 1, z > 0
     copies = Copies()
+    near, far = me.peers()
 
     def got(dst, recv, when=None):
         arrived(dst, local_sem.at[2], recv, me.at_mate(), when)
@@ -108,11 +126,13 @@
     own_local.start()
     fit_local = pltpu.make_async_copy(fit_ref, fit.at[span(z * deep, deep), :], local_sem.at[1])
     fit_local.start()
+    scr_local = pltpu.make_async_copy(scr_any, scr_ref, local_sem.at[3])
+    scr_local.start()
 
     def plane(zz, src, s, when):
-        for j in range(1, chips):
-            _, o, x = me.other(j)
-            copies.start(src, spot(zz, me.o, me.x), plane_sem.at[s, j], o_recv.at[zz, me.o, me.x],
+        for ja, jx in near:
+            _, o, x = me.peer(ja, jx)
+            copies.start(src, spot(zz, me.o, me.x), plane_sem.at[s, ja * me.nx + jx], o_recv.at[zz, me.o, me.x],
                          {"orb": o, "pts": x}, when)
 
     def wait_piece(zz, o, x, when=None):
@@ -136,18 +156,37 @@
         plane(hi, spot(hi, me.o, me.x), 2 * s, in_hi)
 
     for d in range(1, nz):
+        to = lax.rem(z + d, nz)
+        relayed = ((to == nz - 1) & (z == nz - 3)) | ((to == 0) & (z == 2))
         copies.start(fit_ref, fit.at[span(z * deep, deep), :], f_sem.at[d], f_recv.at[z],
-                     {"grid": lax.rem(z + d, nz)})
+                     {"grid": to}, jnp.logical_not(relayed))
+    has_relay_right, has_relay_left = (z == nz - 2) & (z >= 1), (z == 1) & (nz >= 3)
+
+    def relay(origin, to, k, when):
+        src = fit.at[span(origin * deep, deep), :]
+        got(src, f_recv.at[origin], when)
+        copies.start(src, src, relay_sem.at[k], f_recv.at[origin], {"grid": to}, when)
 
     own_local.wait()
     for d in range(nz):
         zz = lax.rem(z + d, nz)
-        for j in range(chips):
-            _, o, x = me.other(j)
-            if j > 0:
+        for ja, jx in [(0, 0)] + near:
+            _, o, x = me.peer(ja, jx)
+            if (ja, jx) != (0, 0):
                 wait_piece(zz, o, x)
             src = spot(zz, o, x)
-            copies.start(src, src, mate_sem.at[d, j], o_recv.at[zz, o, x], me.at_mate())
+            for fa, fx, ka, kx in me.onward(d, ja, jx):
+                _, oo, xx = me.peer(ka, kx)
+                copies.start(src, src, onward_sem.at[d, fa * me.nx + fx], o_recv.at[zz, o, x],
+                             {"orb": oo, "pts": xx})
+            copies.start(src, src, mate_sem.at[d, ja * me.nx + jx], o_recv.at[zz, o, x], me.at_mate())
+    for d in range(nz):
+        zz = lax.rem(z + d, nz)
+        for ja, jx in far:
+            _, o, x = me.peer(ja, jx)
+            wait_piece(zz, o, x)
+            src = spot(zz, o, x)
+            copies.start(src, src, mate_sem.at[d, ja * me.nx + jx], o_recv.at[zz, o, x], me.at_mate())
     for d in range(nz):
         zz = lax.rem(z + d, nz)
         for j in range(chips):
@@ -156,7 +195,7 @@
 
     nrows = full.shape[0]
     npoint, ncol = scr_ref.shape
-    tile = min(512, ncol)
+    tile = min(1024, ncol)
     gtile = min(512, nrows)
     number = me.o * me.nx + me.x
 
@@ -179,7 +218,11 @@
         rows[:, at] = dot(hot, gram[:, at], 1, 0).astype(BF16)
         rows_low[:, at] = dot(hot, low[:, at], 1, 0).astype(BF16)
 
+    if nz >= 3:
+        relay(nz - 3, nz - 1, 0, has_relay_right)
+        relay(2, 0, 1, has_relay_left)
     total[...] = jnp.zeros_like(total)
+    scr_local.wait()
 
     @pl.loop(0, ncol // tile)
     def _(k):
@@ -209,7 +252,8 @@
     for d, zz in order:
         at = span(zz * deep, deep)
         if d < nz:
-            got(fit.at[at, :], f_recv.at[zz])
+            taken = ((zz == nz - 3) & has_relay_right) | ((zz == 2) & has_relay_left)
+            got(fit.at[at, :], f_recv.at[zz], jnp.logical_not(taken))
         else:
             fit_local.wait()
         v_mate[d - 1] = dot(fit[at, :], rows[:, mate_cols], 1, 0).astype(BF16)
@@ -242,10 +286,14 @@
     def piece(zz, c, core):
         return gram.at[span(zz * deep + c * sub, sub), span(core * wide, wide)]
 
-    def pass_on(zz, d, j):
-        c, _, _ = me.other(j)
+    def pass_on(zz, d, ja, jx):
+        c, _, _ = me.peer(ja, jx)
         src = piece(zz, c, me.core)
-        copies.start(src, src, w_m.at[d, j], w_r.at[zz, c, me.core], me.at_mate())
+        for fa, fx, ka, kx in me.onward(d, ja, jx):
+            _, oo, xx = me.peer(ka, kx)
+            copies.start(src, src, w_p.at[d, fa * me.nx + fx], w_r.at[zz, c, me.core],
+                         {"orb": oo, "pts": xx})
+        copies.start(src, src, w_m.at[d, ja * me.nx + jx], w_r.at[zz, c, me.core], me.at_mate())
 
     gram[span(z * deep + me.chip * sub, sub), mine_cols] = value.astype(BF16)
     own_piece = piece(z, me.chip, me.core)
@@ -257,16 +305,17 @@
         src = piece(zz, me.chip, me.core)
         if d > 0:
             got(src, w_r.at[zz, me.chip, me.core])
-        for j in range(1, chips):
-            _, o, x = me.other(j)
-            copies.start(src, src, w_p.at[d, j], w_r.at[zz, me.chip, me.core], {"orb": o, "pts": x})
-        pass_on(zz, d, 0)
-    for d in range(nz):
-        zz = lax.rem(z + d, nz)
-        for j in range(1, chips):
-            c, _, _ = me.other(j)
-            got(piece(zz, c, me.core), w_r.at[zz, c, me.core])
-            pass_on(zz, d, j)
+        for ja, jx in near:
+            _, o, x = me.peer(ja, jx)
+            copies.start(src, src, w_p.at[d, ja * me.nx + jx], w_r.at[zz, me.chip, me.core], {"orb": o, "pts": x})
+        pass_on(zz, d, 0, 0)
+    for group in (near, far):
+        for d in range(nz):
+            zz = lax.rem(z + d, nz)
+            for ja, jx in group:
+                c, _, _ = me.peer(ja, jx)
+                got(piece(zz, c, me.core), w_r.at[zz, c, me.core])
+                pass_on(zz, d, ja, jx)
     for d in range(nz):
         zz = lax.rem(z + d, nz)
         for j in range(chips):
@@ -303,9 +352,10 @@
     results = pl.pallas_call(
         functools.partial(fused, sizes),
         out_shape=outs,
-        in_specs=[vmem] * 4,
+        in_specs=[vmem] * 3 + [pl.BlockSpec(memory_space=pl.ANY)],
         out_specs=(vmem,) * 2,
         scratch_shapes=[
+            pltpu.VMEM((npoint, ncol), BF16),
             pltpu.VMEM((nrows, width), BF16),
             pltpu.VMEM((nrows, npoint), BF16),
             pltpu.VMEM((nrows, nrows), BF16),
@@ -322,7 +372,7 @@
             pltpu.VMEM((nz, sub, wide), BF16),
             pltpu.VMEM((nz, sub, wide), BF16),
             pltpu.VMEM((own, nrows), F32),
-            dma((3,)),
+            dma((4,)),
             dma((nz, no, nx)),
             dma((nz,)),
             dma((nz,)),
@@ -330,6 +380,8 @@
             dma((2 * nz, chips)),
             dma((nz, chips)),
             dma((nz,)),
+            dma((nz, chips)),
+            dma((2,)),
             dma((nz,)),
             dma((nz,)),
             dma((nz, others)),

time: 106 us -> 100 us (0.943)
  the two profiles are of different devices: /device:TPU:19 before, /device:TPU:0 now
where the time goes in v4:
time: 100 us; the launch traced here: 99.3 us
  Pallas kernels  98.6 us (99%)
    pallas_call x1, Pallas kernels, per_device(): pl.pallas_call(functools.partial(fused, sizes), out_shape=outs, in_specs=...  96.6 us
    pallas_call x1, Pallas kernels, per_device(): pl.pallas_call(functools.partial(finish, nrows), out_shape=outs, in_specs...  2.06 us

profile of v4, /device:TPU:0, one launch (start us, length us, event | category | flops | bytes accessed | tf_op | source)
XLA Modules:
  0.0 99.3 jit_solution(12674898792055367905)
XLA Ops:
  0.6 96.6 %shard_map.59 = (f32[256,256]{1,0:T(8,128)}, f32[256,512]{1,0:T(8,128)}) custom-call(bf16[256,512]{1,0:T(8,128)(2,1)} %orb_ref.1, s32[1,8192]{1,0:T(1,128)} %bitcast.1, bf16[256,1024]{1,0:T(8,128)(2,1)} %fit_ref.1, bf16[1024,2048]{1,0:T(8,128)(2,1)} %scr_any.1), custom_call_target="tpu_custom_call" | custom-call | tf_op jit(solution)/shard_map/pallas_call | solution.py:352
  97.2 2.1 %shard_map.60 = (f32[256,256]{1,0:T(8,128)}, f32[256,512]{1,0:T(8,128)}) custom-call(f32[256,256]{1,0:T(8,128)} %get-tuple-element.4.terms_ref, f32[256,512]{1,0:T(8,128)} %get-tuple-element.5.matrix_ref), custom_call_target="tpu_custom_call" | custom-call | tf_op jit(solution)/shard_map/pallas_call | solution.py:400
